TPU v7x, 256 devices: a whole 4x4x8 slice. The times are simulated.
256 devices in a mesh: row: 16 (over y_lo, z), col: 16 (over y_hi, x, core).
Axes of the slice: x: 4, y: 4 (y_hi: 2, y_lo: 2; y = y_hi * 2 + y_lo), z: 8, core: 2. Of those that a mesh axis runs over, the one named last changes fastest.
Arguments:
- env: float32 [1024, 32768], P('row', 'col'), may hold values from -0.03125 to 0.03125
- wave: float32 [32768, 2048], P('row', 'col'), may hold values from -6 to 6
- mpo: float32 [16, 16], replicated, may hold values from -1.5 to 1.5
Outputs:
- applied: float32 [1024, 2048], P('row', 'col')
All inputs are finite; a program needn't handle non-finite values.
Results may differ from a plain program's by a relative error of at most 0.00007.
Values sent between devices are 32-bit elements; how exact they have to be, the bound alone decides.
A program may use at most 128 MiB of HBM per device.

v0:
```python
import jax
import jax.numpy as jnp
from jax import lax
from jax.sharding import PartitionSpec as P


def shards(env, wave, mpo):
    spins = mpo.shape[0]
    env_full = lax.all_gather(env, "col", axis=1, tiled=True)
    left_local = wave.shape[0]
    right_local = wave.shape[1] // spins
    wave3 = wave.reshape(left_local, right_local, spins)
    mixed = jnp.einsum("krs,st->ktr", wave3, mpo, precision=lax.Precision.HIGHEST)
    spun = lax.all_to_all(mixed, "col", split_axis=1, concat_axis=2, tiled=True)
    flat = spun.reshape(left_local, -1)
    return jnp.dot(
        env_full,
        lax.all_gather(flat, "row", axis=0, tiled=True),
        precision=lax.Precision.HIGHEST,
        preferred_element_type=jnp.float32,
    )


def solution(mesh):
    in_specs = (P("row", "col"), P("row", "col"), P())
    out_specs = P("row", "col")
    return jax.shard_map(shards, mesh=mesh, in_specs=in_specs, out_specs=out_specs, check_vma=False)
```

profile of v0, /device:TPU:1, one launch (start us, length us, event | category | flops | bytes accessed | tf_op | source)
XLA Modules:
  0.0 309.1 jit_solution(15223084674707760075)
XLA Ops:
  6.5 0.0 copy-start
  6.5 0.0 all-gather.5.cloned.1.call-start
  6.5 0.7 all-gather.5.cloned.1.call-update
  7.3 0.0 all-gather.3.cloned.1.call-start
  7.3 1.6 copy.9
  8.9 0.0 copy-done
  8.9 1.0 convolution_bitcast_fusion
  9.9 0.6 copy.11
  10.6 26.5 %all_to_all.4 = f32[2048,16,8]{0,2,1:T(8,128)} all-to-all(f32[2048,16,8]{0,2,1:T(8,128)S(1)} %copy.11), channel_id=1, replica_groups=mesh['row'=16,'col'=16] {'col'}, dimensions={1} | all-to-all | bytes 2097152 | tf_op jit(solution)/shard_map/all_to_all | solution.py:14
  37.1 0.0 all-gather.3.cloned.1.call-update
  37.1 58.9 %all-gather.5.cloned.1.call-done = f32[64,32768]{1,0:T(8,128)} async-done(((f32[64,2048]{1,0:T(8,128)}), f32[64,32768]{1,0:T(8,128)}) %all-gather.5.cloned.1.call-update) | async-done | bytes 8388624 | tf_op jit(solution)/shard_map/all_gather | solution.py:9
  96.0 184.5 %all-gather.3.cloned.1.call-done = f32[32768,128]{0,1:T(8,128)} async-done(((f32[2048,128]{0,1:T(8,128)}), f32[32768,128]{0,1:T(8,128)}) %all-gather.3.cloned.1.call-update) | async-done | bytes 16777232 | tf_op jit(solution)/shard_map/all_gather | solution.py:18
  280.5 21.7 %convolution_bitcast_fusion.1 = f32[64,128]{1,0:T(8,128)} fusion(f32[32768,128]{0,1:T(8,128)} %all-gather.3.cloned.1.call-done, f32[64,32768]{1,0:T(8,128)} %all-gather.5.cloned.1.call-done), kind=kOutput, calls=%fused_computation.1 | convolution fusion | flops 3221225472 | bytes 25198592 | tf_op jit(solution)/shard_map/dot_general | solution.py:16
Async XLA Ops:
  6.5 2.3 copy-start
  6.5 89.4 %all-gather.5.cloned.1.call-start = ((), (), s32[]{:S(2)}) async-start(), calls=%async_computation.2 | async-start | bytes 8912896 | tf_op jit(solution)/shard_map/all_gather | solution.py:9
  7.3 273.3 %all-gather.3.cloned.1.call-start = ((), (), s32[]{:S(2)}) async-start(), calls=%async_computation.1 | async-start | bytes 17825792 | tf_op jit(solution)/shard_map/all_gather | solution.py:18
Sparse Core Ops, SparseCore 0:
  10.1 85.8 all-gather.4
  97.8 182.7 all-gather.2
where the time goes:
time: 309 us
  waiting for transfers between devices  244 us (79%)
  blocking collectives  26.5 us (9%)
  matrix products  22.8 us (7%)
  between operations  13.4 us (4%)
    all_gather x1, waiting for transfers between devices, shards(): lax.all_gather(flat, 'row', axis=0, tiled=True)  185 us
    all_gather x1, waiting for transfers between devices, shards(): env_full = lax.all_gather(env, 'col', axis=1, tiled=True)  58.9 us
    all_to_all x1, blocking collectives, shards(): spun = lax.all_to_all(mixed, 'col', split_axis=1, concat_axis=2, tiled=True)  26.5 us
    dot_general x1, matrix products, shards(): jnp.dot(env_full, lax.all_gather(flat, 'row', axis=0, tiled=True), precis...  21.7 us
  transfers between devices with their start and end apart: 2, of which 2 were waited for; matrix products, arithmetic and copies ran while one was open for 1% of the time, Pallas kernels for 0%

commit v1 on v0

v1 whole, which is shorter than its diff:
```python
import jax
import jax.numpy as jnp
from jax import lax
from jax.sharding import PartitionSpec as P


def shards(env, wave, mpo):
    n = lax.axis_size("row")
    spins = mpo.shape[0]
    swap = [(a * n + b, b * n + a) for a in range(n) for b in range(n)]
    moved = lax.ppermute(env, ("row", "col"), swap)
    env_k = lax.all_gather(moved, "col", axis=0, tiled=True)
    part = jnp.dot(env_k, wave, precision=lax.Precision.HIGHEST, preferred_element_type=jnp.float32)
    block = lax.psum_scatter(part, "row", scatter_dimension=0, tiled=True)
    rows = block.shape[0]
    mixed = jnp.einsum("irs,st->tir", block.reshape(rows, -1, spins), mpo, precision=lax.Precision.HIGHEST)
    spun = lax.all_to_all(mixed, "col", split_axis=0, concat_axis=2, tiled=True)
    return spun.reshape(rows, -1)


def solution(mesh):
    in_specs = (P("row", "col"), P("row", "col"), P())
    out_specs = P("row", "col")
    return jax.shard_map(shards, mesh=mesh, in_specs=in_specs, out_specs=out_specs, check_vma=False)
```

time: 309 us -> 233 us (0.75)
  waiting for transfers between devices: 244 us -> 174 us
  matrix products: 22.8 us -> 10 us
  starting transfers between devices: 0.04 us -> 5.1 us
    all_gather x2 -> x1, waiting for transfers between devices: 243 us -> 109 us  [shards(): env_k = lax.all_gather(moved, 'col', axis=0, tiled=True)]
    reduce_scatter x0 -> x1, waiting for transfers between devices: none -> 56.2 us  [shards(): block = lax.psum_scatter(part, 'row', scatter_dimension=0, tiled=True)]
    dot_general x2, matrix products: 22.8 us -> 10 us  [the longest x1 9.75 us: shards(): jnp.dot(env_k, wave, precision=lax.Precision.HIGHEST, preferred_element_t...]
    ppermute x0 -> x1, waiting for transfers between devices: none -> 9.1 us  [shards(): moved = lax.ppermute(env, ('row', 'col'), swap)]
    ppermute x0 -> x1, starting transfers between devices: none -> 5.05 us  [shards(): moved = lax.ppermute(env, ('row', 'col'), swap)]
  transfers between devices with their start and end apart: 2 -> 3, of which waited for: 2 -> 3; matrix products, arithmetic and copies ran while one was open for 1% -> 0% of each run, Pallas kernels for 0% -> 0%
where the time goes in v1:
time: 233 us
  waiting for transfers between devices  174 us (75%)
  blocking collectives  26 us (11%)
  between operations  13.5 us (6%)
  matrix products  10 us (4%)
  starting transfers between devices  5.1 us (2%)
  local copies, waits for them, and re-layouts  3.12 us (1%)
    all_gather x1, waiting for transfers between devices, shards(): env_k = lax.all_gather(moved, 'col', axis=0, tiled=True)  109 us
    reduce_scatter x1, waiting for transfers between devices, shards(): block = lax.psum_scatter(part, 'row', scatter_dimension=0, tiled=True)  56.2 us
    all_to_all x1, blocking collectives, shards(): spun = lax.all_to_all(mixed, 'col', split_axis=0, concat_axis=2, tiled=True)  26 us
    dot_general x1, matrix products, shards(): jnp.dot(env_k, wave, precision=lax.Precision.HIGHEST, preferred_element_t...  9.75 us
    ppermute x1, waiting for transfers between devices, shards(): moved = lax.ppermute(env, ('row', 'col'), swap)  9.1 us
    ppermute x1, starting transfers between devices, shards(): moved = lax.ppermute(env, ('row', 'col'), swap)  5.05 us
  transfers between devices with their start and end apart: 3, of which 3 were waited for; matrix products, arithmetic and copies ran while one was open for 0% of the time, Pallas kernels for 0%

profile of v1, /device:TPU:1, one launch (start us, length us, event | category | flops | bytes accessed | tf_op | source)
XLA Modules:
  0.0 232.7 jit_solution(1275761468202975840)
XLA Ops:
  6.5 0.0 copy-start
  6.5 0.0 copy-start.2
  6.5 0.0 all-gather.2.cloned.1.call-start
  6.5 5.1 %collective-permute-start = (f32[64,2048]{1,0:T(8,128)}, f32[64,2048]{1,0:T(8,128)S(1)}, u32[]{:S(2)}, u32[]{:S(2)}) collective-permute-start(f32[64,2048]{1,0:T(8,128)} %param.3), channel_id=1, source_target_pairs={{0,0},{1,16},{2,32},{3,48},{4,64},{5,80},{6,96},{7,112},{8,128},{9... | collective-permute-start | bytes 1572872 | tf_op jit(solution)/shard_map/ppermute | solution.py:11
  11.6 9.1 %collective-permute-done = f32[64,2048]{1,0:T(8,128)S(1)} collective-permute-done((f32[64,2048]{1,0:T(8,128)}, f32[64,2048]{1,0:T(8,128)S(1)}, u32[]{:S(2)}, u32[]{:S(2)}) %collective-permute-start) | collective-permute-done | bytes 524320 | tf_op jit(solution)/shard_map/ppermute | solution.py:11
  20.7 0.0 copy-start.1
  20.7 0.8 copy-done.1
  21.6 0.0 all-gather.2.cloned.1.call-update
  21.6 0.0 reduce-scatter.2.cloned.1.call-start
  21.6 108.9 %all-gather.2.cloned.1.call-done = f32[1024,2048]{1,0:T(8,128)} async-done(((f32[64,2048]{1,0:T(8,128)}), f32[1024,2048]{1,0:T(8,128)}) %all-gather.2.cloned.1.call-update) | async-done | bytes 8388624 | tf_op jit(solution)/shard_map/all_gather | solution.py:12
  130.5 0.0 copy-done
  130.5 9.7 %fusion.1 = f32[1024,128]{1,0:T(8,128)} fusion(f32[1024,2048]{1,0:T(8,128)} %all-gather.2.cloned.1.call-done, f32[2048,128]{1,0:T(8,128)S(1)} %copy-done), kind=kOutput, calls=%fused_computation.4 | convolution fusion | flops 3221225472 | bytes 9961472 | tf_op jit(solution)/shard_map/dot_general | solution.py:13
  140.3 0.0 reduce-scatter.2.cloned.1.call-update
  140.3 56.2 %reduce-scatter.2.cloned.1.call-done = f32[64,128]{1,0:T(8,128)} async-done(((f32[1024,128]{1,0:T(8,128)}), f32[64,128]{1,0:T(8,128)}) %reduce-scatter.2.cloned.1.call-update) | async-done | bytes 32784 | tf_op jit(solution)/shard_map/reduce_scatter | solution.py:14
  196.5 0.8 copy.10
  197.4 0.0 copy-done.2
  197.4 0.3 convolution_bitcast_fusion
  197.7 0.1 reshape.10
  197.8 26.0 %all_to_all.15 = f32[16,1,512]{2,1,0:T(1,128)S(1)} all-to-all(f32[16,1,512]{2,1,0:T(1,128)S(1)} %reshape.10), channel_id=1, replica_groups=mesh['row'=16,'col'=16] {'col'}, dimensions={0} | all-to-all | bytes 65536 | tf_op jit(solution)/shard_map/all_to_all | solution.py:17
  223.8 0.5 broadcast
  224.3 0.7 reduce
  225.1 0.1 reshape.11
  225.2 0.7 copy.13
  (2 shorter events, 0.0 us)
Async XLA Ops:
  6.5 124.0 %copy-start = (f32[2048,128]{1,0:T(8,128)S(1)}, f32[2048,128]{1,0:T(8,128)}, u32[]{:S(2)}) copy-start(f32[2048,128]{1,0:T(8,128)} %param.4) | copy-start | bytes 3145732
  6.5 190.9 %copy-start.2 = (f32[16,16]{1,0:T(8,128)S(1)}, f32[16,16]{1,0:T(8,128)}, u32[]{:S(2)}) copy-start(f32[16,16]{1,0:T(8,128)} %param.5) | copy-start | bytes 3076
  6.5 124.0 %all-gather.2.cloned.1.call-start = ((), (), s32[]{:S(2)}) async-start(), calls=%async_computation.2 | async-start | bytes 8912896 | tf_op jit(solution)/shard_map/all_gather | solution.py:12
  6.5 14.2 %collective-permute-start = (f32[64,2048]{1,0:T(8,128)}, f32[64,2048]{1,0:T(8,128)S(1)}, u32[]{:S(2)}, u32[]{:S(2)}) collective-permute-start(f32[64,2048]{1,0:T(8,128)} %param.3), channel_id=1, source_target_pairs={{0,0},{1,16},{2,32},{3,48},{4,64},{5,80},{6,96},{7,112},{8,128},{9... | collective-permute-start | bytes 1572872 | tf_op jit(solution)/shard_map/ppermute | solution.py:11
  20.7 0.8 copy-start.1
  21.6 175.0 %reduce-scatter.2.cloned.1.call-start = ((), (), s32[]{:S(2)}) async-start(), calls=%async_computation.3 | async-start | bytes 557056 | tf_op jit(solution)/shard_map/reduce_scatter | solution.py:14
Sparse Core Ops, SparseCore 0:
  21.7 108.7 all-gather.1
  140.4 56.0 reduce-scatter.1

commit v2 on v1

v2 whole, which is shorter than its diff:
```python
import functools

import jax
import jax.numpy as jnp
from jax import lax
from jax.experimental import pallas as pl
from jax.experimental.pallas import tpu as pltpu
from jax.sharding import PartitionSpec as P

MESH = pl.DeviceIdType.MESH
CHUNKS = 4
X, Z = 4, 8


def device(yh, yl, x, z, core):
    return (yl * Z + z, yh * 2 * X + x * 2 + core)


def split(value):
    high = value.astype(jnp.bfloat16)
    return high, (value - high.astype(jnp.float32)).astype(jnp.bfloat16)


def dot(a, b):
    return jnp.dot(a, b, preferred_element_type=jnp.float32)


def kernel(
    env, wave, mpo, out, spread, gathered, waves, wave_high, wave_low, part, other, summed, landed, mixed, final,
    a_send, a_recv, b_send, b_recv, w_send, w_recv, w_local, g_send, g_recv, c_send, c_recv,
    y_send, y_recv, z_send, z_recv, f_send, f_recv,
):
    row, col = lax.axis_index("row"), lax.axis_index("col")
    yl, z = row // Z, row % Z
    yh, x, core = col // (2 * X), (col // 2) % X, col % 2
    chunks, n, height, _ = summed.shape

    def remote(src, dst, send, recv, to):
        return pltpu.make_async_remote_copy(
            src_ref=src, dst_ref=dst, send_sem=send, recv_sem=recv, device_id=to, device_id_type=MESH
        )

    def wait(ref, sem):
        pltpu.make_async_copy(ref, ref, sem).wait()

    right = device(yh, yl, (x + 1) % X, z, core)
    left = device(yh, yl, (x + X - 1) % X, z, core)
    sibling = device(yh, yl, x, z, 1 - core)
    across = device(1 - yh, yl, x, z, core)

    barrier = pltpu.get_barrier_semaphore()

    def greet(to):
        pl.semaphore_signal(barrier, inc=1, device_id=to, device_id_type=MESH)

    for step in range(1, X):
        greet(device(yh, yl, (x + step) % X, z, core))
    greet(sibling)
    greet(across)
    source = yl * 2 * X + x * 2 + z % 2

    @pl.loop(0, n)
    def _(j):
        greet((j, source))

    @pl.loop(1, n)
    def _(j):
        greet(((row + j) % n, col))
        greet((row, (col + j) % n))

    own_wave = pltpu.make_async_copy(wave.at[:, yh], waves.at[yh], w_local)
    own_wave.start()

    spins = mpo.shape[0]
    size = mixed.shape[0] * mixed.shape[1]
    rights = size // spins
    wide = lax.broadcasted_iota(jnp.int32, (size, spins), 0)
    pick_t = (wide // rights == lax.broadcasted_iota(jnp.int32, (size, spins), 1)).astype(jnp.float32)
    tall = lax.broadcasted_iota(jnp.int32, (spins, size), 1)
    pick_s = (tall % spins == lax.broadcasted_iota(jnp.int32, (spins, size), 0)).astype(jnp.float32)
    by_t = lax.dot_general(
        pick_t, mpo[...], (((1,), (1,)), ((), ())), precision=lax.Precision.HIGHEST,
        preferred_element_type=jnp.float32,
    )
    full = jnp.dot(by_t, pick_s, precision=lax.Precision.HIGHEST, preferred_element_type=jnp.float32)
    same = (
        lax.broadcasted_iota(jnp.int32, (size, size), 0) % rights
        == lax.broadcasted_iota(jnp.int32, (size, size), 1) // spins
    )
    mixing = jnp.where(same, full, 0.0)

    pl.semaphore_wait(barrier, (X - 1) + 2 + n + 2 * (n - 1))

    wide_k = spread.shape[3]

    def slices(h, to_x):
        return env.at[pl.ds(h * height, height), pl.ds(pl.multiple_of(to_x * wide_k, wide_k), wide_k)]

    for h in range(chunks):
        for step in range(1, X):
            to_x = (x + step) % X
            remote(
                slices(h, to_x), spread.at[h, x], a_send.at[h], a_recv.at[h], device(yh, yl, to_x, z, core)
            ).start()
        pltpu.make_async_copy(slices(h, x), spread.at[h, x], a_recv.at[h]).start()
    crossing = remote(wave.at[:, 1 - yh], waves.at[yh], w_send, w_recv, across)
    crossing.start()

    has_self = (yl == yh) & (z % 2 == core)

    def forward(h):
        wait(spread.at[h], a_recv.at[h])

        @pl.loop(0, n)
        def _(i):
            j = (i + row) % n
            from_x, to_yh, to_core = j // 4, (j // 2) % 2, j % 2
            src = spread.at[h, from_x, :, pl.ds(pl.multiple_of((j % 4) * 128, 128), 128)]
            dst = gathered.at[h, 2 * x + to_core, row]
            to = device(to_yh, yh, x, 2 * from_x + core, to_core)
            here = has_self & (to_yh == yh) & (2 * from_x + core == z) & (to_core == core)

            @pl.when(jnp.logical_not(here))
            def _():
                remote(src, dst, b_send.at[h], b_recv.at[h], to).start()

            @pl.when(here)
            def _():
                pltpu.make_async_copy(src, dst, b_recv.at[h]).start()

    mine, from_left, from_right, far = (2 * ((x + s) % X) + core for s in (0, 3, 1, 2))
    half = n // 2

    def gather_own(h):
        wait(gathered.at[h, mine], b_recv.at[h])
        own = gathered.at[h, mine]
        remote(own, own, g_send.at[h, 0], g_recv.at[h, 0], right).start()
        remote(own, own, g_send.at[h, 1], g_recv.at[h, 1], left).start()
        remote(own, own, c_send.at[h, 0], c_recv.at[h, 0], sibling).start()

    def gather_relay(h):
        got = gathered.at[h, from_left]
        wait(got, g_recv.at[h, 0])
        low = gathered.at[h, from_left, pl.ds(0, half)]
        remote(low, low, g_send.at[h, 2], g_recv.at[h, 2], right).start()
        remote(got, got, c_send.at[h, 1], c_recv.at[h, 1], sibling).start()
        got = gathered.at[h, from_right]
        wait(got, g_recv.at[h, 1])
        high = gathered.at[h, from_right, pl.ds(half, half)]
        remote(high, high, g_send.at[h, 3], g_recv.at[h, 3], left).start()
        remote(got, got, c_send.at[h, 2], c_recv.at[h, 2], sibling).start()

    def gather_end(h):
        wait(gathered.at[h, far, pl.ds(0, half)], g_recv.at[h, 2])
        wait(gathered.at[h, far, pl.ds(half, half)], g_recv.at[h, 3])
        got = gathered.at[h, far]
        remote(got, got, c_send.at[h, 3], c_recv.at[h, 3], sibling).start()

    def wave_ready():
        own_wave.wait()
        crossing.wait_recv()
        for p in range(X):
            high, low = split(jnp.concatenate([waves[0, p], waves[1, p]], axis=1))
            wave_high[p] = high
            wave_low[p] = low

    def multiply(h):
        for s in range(4):
            wait(gathered.at[h, s], c_recv.at[h, s])
        total = None
        for p in range(X):
            block = jnp.concatenate(
                [gathered[h, 2 * p].reshape(n * height, 128), gathered[h, 2 * p + 1].reshape(n * height, 128)], axis=1
            )
            high, low = split(block)
            term = dot(high, wave_high[p]) + dot(high, wave_low[p]) + dot(low, wave_high[p])
            total = term if total is None else total + term
        part[h, 0] = total[:, :128].reshape(n, height, 128)
        part[h, 1] = total[:, 128:].reshape(n, height, 128)
        remote(part.at[h, 1 - yh], other.at[h], y_send.at[h], y_recv.at[h], across).start()

    def reduce(h):
        wait(other.at[h], y_recv.at[h])
        summed[h] = part[h, yh] + other[h]

        @pl.loop(1, n)
        def _(j):
            to = (row + j) % n
            remote(summed.at[h, to], landed.at[h, j - 1], z_send.at[h], z_recv.at[h], (to, col)).start()

    stages = (gather_own, gather_relay, gather_end, multiply, reduce)
    for h in range(chunks):
        forward(h)
    for step in range(chunks + len(stages) - 1):
        for s, stage in enumerate(stages):
            h = step - s
            if 0 <= h < chunks:
                if stage is multiply and h == 0:
                    wave_ready()
                stage(h)

    rows = []
    for h in range(chunks):
        wait(landed.at[h], z_recv.at[h])
        rows.append(summed[h, row] + jnp.sum(landed[h], axis=0))
    block = jnp.concatenate(rows + [jnp.zeros((128 - chunks * height, 128), jnp.float32)], axis=0)
    turned = lax.dot_general(
        mixing, block, (((1,), (1,)), ((), ())), precision=lax.Precision.HIGHEST, preferred_element_type=jnp.float32
    )
    mixed[...] = turned.reshape(mixed.shape)

    @pl.loop(1, n)
    def _(j):
        to = (col + j) % n
        remote(mixed.at[to], final.at[col], f_send, f_recv, (row, to)).start()

    final[col] = mixed[col]
    wait(final.at[pl.ds(0, n - 1)], f_recv)
    out[...] = final[...].reshape(size, 128).T[: chunks * height]

    wait(final.at[pl.ds(0, n - 1)], f_send)
    crossing.wait_send()
    for h in range(chunks):
        wait(spread.at[h, pl.ds(0, X - 1)], a_send.at[h])

        @pl.when(has_self)
        def _():
            wait(gathered.at[h, 0, pl.ds(0, n - 1)], b_send.at[h])

        @pl.when(jnp.logical_not(has_self))
        def _():
            wait(gathered.at[h, 0], b_send.at[h])

        for s in range(2):
            wait(gathered.at[h, 0], g_send.at[h, s])
            wait(gathered.at[h, 0, pl.ds(0, half)], g_send.at[h, 2 + s])
        for s in range(4):
            wait(gathered.at[h, 0], c_send.at[h, s])
        wait(other.at[h], y_send.at[h])
        wait(landed.at[h], z_send.at[h])


def shards(env, wave, mpo):
    n = lax.axis_size("row")
    rows, depth = env.shape
    height = rows // CHUNKS
    wave4 = wave.reshape(X, 2, depth // (2 * X), wave.shape[1])
    f32, bf16 = jnp.float32, jnp.bfloat16
    dma = pltpu.SemaphoreType.DMA
    h = CHUNKS
    return pl.pallas_call(
        kernel,
        out_shape=jax.ShapeDtypeStruct((rows, 128), f32),
        in_specs=[
            pl.BlockSpec(memory_space=pl.ANY),
            pl.BlockSpec(memory_space=pl.ANY),
            pl.BlockSpec(memory_space=pltpu.VMEM),
        ],
        out_specs=pl.BlockSpec(memory_space=pltpu.VMEM),
        scratch_shapes=[
            pltpu.VMEM((h, X, height, depth // X), f32),
            pltpu.VMEM((h, 2 * X, n, height, 128), f32),
            pltpu.VMEM((2, X, depth // (2 * X), 128), f32),
            pltpu.VMEM((X, depth // (2 * X), 256), bf16),
            pltpu.VMEM((X, depth // (2 * X), 256), bf16),
            pltpu.VMEM((h, 2, n, height, 128), f32),
            pltpu.VMEM((h, n, height, 128), f32),
            pltpu.VMEM((h, n, height, 128), f32),
            pltpu.VMEM((h, n - 1, height, 128), f32),
            pltpu.VMEM((n, 8, 128), f32),
            pltpu.VMEM((n, 8, 128), f32),
            dma((h,)), dma((h,)), dma((h,)), dma((h,)), dma, dma, dma, dma((h, 4)), dma((h, 4)), dma((h, 4)), dma((h, 4)),
            dma((h,)), dma((h,)), dma((h,)), dma((h,)), dma, dma,
        ],
        compiler_params=pltpu.CompilerParams(
            collective_id=0, has_side_effects=True, vmem_limit_bytes=40 * 1024 * 1024
        ),
    )(env, wave4, mpo)


def solution(mesh):
    in_specs = (P("row", "col"), P("row", "col"), P())
    out_specs = P("row", "col")
    return jax.shard_map(shards, mesh=mesh, in_specs=in_specs, out_specs=out_specs, check_vma=False)
```

time: 233 us -> 84.7 us (0.36)
  waiting for transfers between devices: 174 us -> 0 us
  Pallas kernels: 0 us -> 80.9 us
  blocking collectives: 26 us -> 0 us
  between operations: 13.5 us -> 0.01 us
  matrix products: 10 us -> 0 us
  starting transfers between devices: 5.1 us -> 0 us
    all_gather x1 -> x0, waiting for transfers between devices: 109 us -> none  [shards(): env_k = lax.all_gather(moved, 'col', axis=0, tiled=True)]
    pallas_call x0 -> x1, Pallas kernels: none -> 80.9 us  [shards(): pl.pallas_call(kernel, out_shape=jax.ShapeDtypeStruct((rows, 128), f32),...]
    reduce_scatter x1 -> x0, waiting for transfers between devices: 56.2 us -> none  [shards(): block = lax.psum_scatter(part, 'row', scatter_dimension=0, tiled=True)]
    all_to_all x1 -> x0, blocking collectives: 26 us -> none  [shards(): spun = lax.all_to_all(mixed, 'col', split_axis=0, concat_axis=2, tiled=True)]
    dot_general x2 -> x0, matrix products: 10 us -> none  [the longest x1 9.75 us: shards(): jnp.dot(env_k, wave, precision=lax.Precision.HIGHEST, preferred_element_t...]
    ppermute x1 -> x0, waiting for transfers between devices: 9.1 us -> none  [shards(): moved = lax.ppermute(env, ('row', 'col'), swap)]
    ppermute x1 -> x0, starting transfers between devices: 5.05 us -> none  [shards(): moved = lax.ppermute(env, ('row', 'col'), swap)]
    unnamed x8 -> x7, local copies, waits for them, and re-layouts: 1.03 us -> 3.58 us
  transfers between devices with their start and end apart: 3 -> 0, of which waited for: 3 -> 0; matrix products, arithmetic and copies ran while one was open for 0% -> 0% of each run, Pallas kernels for 0% -> 0%
where the time goes in v2:
time: 84.7 us; the launch traced here: 84.5 us
  Pallas kernels  80.9 us (96%)
  local copies, waits for them, and re-layouts  3.58 us (4%)
    pallas_call x1, Pallas kernels, shards(): pl.pallas_call(kernel, out_shape=jax.ShapeDtypeStruct((rows, 128), f32),...  80.9 us
    unnamed x7, local copies, waits for them, and re-layouts  3.58 us

profile of v2, /device:TPU:1, one launch (start us, length us, event | category | flops | bytes accessed | tf_op | source)
XLA Modules:
  0.0 84.5 jit_solution(13090390054486979300)
XLA Ops:
  0.0 0.0 copy-start
  0.0 1.2 %copy-done = f32[2048,128]{1,0:T(8,128)S(1)} copy-done((f32[2048,128]{1,0:T(8,128)S(1)}, f32[2048,128]{1,0:T(8,128)}, u32[]{:S(2)}) %copy-start) | copy-done | bytes 1048600
  1.2 0.0 copy-start.1
  1.2 1.0 %copy-done.1 = f32[64,2048]{1,0:T(8,128)S(1)} copy-done((f32[64,2048]{1,0:T(8,128)S(1)}, f32[64,2048]{1,0:T(8,128)}, u32[]{:S(2)}) %copy-start.1) | copy-done | bytes 524312
  2.3 0.0 copy-start.2
  2.3 0.7 copy-done.2
  3.0 80.9 %shard_map.37 = f32[64,128]{1,0:T(8,128)S(1)} custom-call(f32[64,2048]{1,0:T(8,128)S(1)} %copy-done.1, f32[4,2,256,128]{3,2,1,0:T(8,128)S(1)} %bitcast.1, f32[16,16]{1,0:T(8,128)S(1)} %copy-done.2), custom_call_target="tpu_custom_call" | custom-call | tf_op jit(solution)/shard_map/pallas_call | solution.py:251
  83.8 0.6 copy.5
Async XLA Ops:
  0.0 1.2 %copy-start = (f32[2048,128]{1,0:T(8,128)S(1)}, f32[2048,128]{1,0:T(8,128)}, u32[]{:S(2)}) copy-start(f32[2048,128]{1,0:T(8,128)} %param.4) | copy-start | bytes 3145732
  1.2 1.0 %copy-start.1 = (f32[64,2048]{1,0:T(8,128)S(1)}, f32[64,2048]{1,0:T(8,128)}, u32[]{:S(2)}) copy-start(f32[64,2048]{1,0:T(8,128)} %env.1) | copy-start | bytes 1572868
  2.3 0.7 copy-start.2

commit v3 on v2

v3 whole, which is shorter than its diff:
```python
import functools

import jax
import jax.numpy as jnp
from jax import lax
from jax.experimental import pallas as pl
from jax.experimental.pallas import tpu as pltpu
from jax.sharding import PartitionSpec as P

MESH = pl.DeviceIdType.MESH
CHUNKS = 4
DIRECT = True
TRUNC = False
GATE_A = True
GATE_B = True
GATE_O = True
ORDER = (
    "A0", "W0", "W1", "W2", "W3", "S0", "A1", "B0", "A2",
    "A3", "B1", "O0", "B2", "O1", "B3", "S1", "V0", "O2",
    "M0", "O3", "M1", "R0", "M2", "R1", "M3", "R2", "R3",
)
X, Z = 4, 8


def device(yh, yl, x, z, core):
    return (yl * Z + z, yh * 2 * X + x * 2 + core)


def split(value):
    high = value.astype(jnp.bfloat16)
    return high, (value - high.astype(jnp.float32)).astype(jnp.bfloat16)


def dot(a, b):
    return jnp.dot(a, b, preferred_element_type=jnp.float32)


def kernel(
    env, wave, mpo, out, spread, gathered, waves, wave_high, wave_low, part, other, summed, landed, mixed, final, table,
    a_send, a_recv, b_send, b_recv, w_send, w_recv, s_send, s_recv, g_send, g_recv, y_send, y_recv, z_send, z_recv,
    f_send, f_recv, w_local, t_local,
):
    row, col = lax.axis_index("row"), lax.axis_index("col")
    yl, z = row // Z, row % Z
    yh, x, core = col // (2 * X), (col // 2) % X, col % 2
    chunks, n, height, _ = landed.shape

    def remote(src, dst, send, recv, to):
        return pltpu.make_async_remote_copy(
            src_ref=src, dst_ref=dst, send_sem=send, recv_sem=recv, device_id=to, device_id_type=MESH
        )

    def wait(ref, sem):
        pltpu.make_async_copy(ref, ref, sem).wait()

    right = device(yh, yl, (x + 1) % X, z, core)
    left = device(yh, yl, (x + X - 1) % X, z, core)
    opposite = device(yh, yl, (x + 2) % X, z, core)
    sibling = device(yh, yl, x, z, 1 - core)
    across = device(1 - yh, yl, x, z, core)

    barrier = pltpu.get_barrier_semaphore()

    def greet(to):
        pl.semaphore_signal(barrier, inc=1, device_id=to, device_id_type=MESH)

    for step in range(1, X):
        greet(device(yh, yl, (x + step) % X, z, core))
    greet(sibling)
    greet(across)
    source = yl * 2 * X + x * 2 + z % 2
    reducer = yh * 2 * X + x * 2 + row % 2

    @pl.loop(0, n // 2)
    def _(j):
        greet((2 * j + core, source))

    @pl.loop(0, n)
    def _(j):
        greet((j, reducer))

    @pl.loop(1, n)
    def _(j):
        greet((row, (col + j) % n))

    own_table = pltpu.make_async_copy(mpo, table, t_local)
    own_table.start()
    own_wave = pltpu.make_async_copy(wave.at[:, yh], waves.at[yh, core], w_local)
    own_wave.start()

    own_table.wait()
    spins = mpo.shape[0]
    size = mixed.shape[0] * mixed.shape[1]
    rights = size // spins
    wide = lax.broadcasted_iota(jnp.int32, (size, spins), 0)
    pick_t = (wide // rights == lax.broadcasted_iota(jnp.int32, (size, spins), 1)).astype(jnp.float32)
    tall = lax.broadcasted_iota(jnp.int32, (spins, size), 1)
    pick_s = (tall % spins == lax.broadcasted_iota(jnp.int32, (spins, size), 0)).astype(jnp.float32)
    by_t = lax.dot_general(
        pick_t, table[...], (((1,), (1,)), ((), ())), precision=lax.Precision.HIGHEST,
        preferred_element_type=jnp.float32,
    )
    full = jnp.dot(by_t, pick_s, precision=lax.Precision.HIGHEST, preferred_element_type=jnp.float32)
    same = (
        lax.broadcasted_iota(jnp.int32, (size, size), 0) % rights
        == lax.broadcasted_iota(jnp.int32, (size, size), 1) // spins
    )
    mixing = jnp.where(same, full, 0.0)

    pl.semaphore_wait(barrier, (X - 1) + 2 + n // 2 + n + (n - 1))

    wide_k = spread.shape[3]

    def slices(h, to_x):
        return env.at[pl.ds(h * height, height), pl.ds(pl.multiple_of(to_x * wide_k, wide_k), wide_k)]

    owed = {}

    def settle(*keys):
        for key in keys:
            if key in owed:
                owed.pop(key)()

    def start(key, src, dst, send, recv, to, landing=None):
        remote(src, dst, send, recv, to).start()
        owed[("sent", *key)] = lambda: wait(src, send)
        owed[("got", *key)] = lambda: wait(dst if landing is None else landing, recv)

    def spread_out(h):
        if GATE_A:
            settle(("sent", "a", h - 1))
        for step in range(1, X):
            to_x = (x + step) % X
            to = device(yh, yl, to_x, z, core)
            remote(slices(h, to_x), spread.at[h, x], a_send.at[h], a_recv.at[h], to).start()
        pltpu.make_async_copy(slices(h, x), spread.at[h, x], a_recv.at[h]).start()
        owed["sent", "a", h] = lambda: wait(spread.at[h, pl.ds(0, X - 1)], a_send.at[h])
        owed["got", "a", h] = lambda: wait(spread.at[h], a_recv.at[h])

    def cross(p):
        dst = waves.at[yh, core, p]
        start(("w", p), wave.at[p, 1 - yh], dst, w_send.at[p], w_recv.at[p], across, waves.at[1 - yh, core, p])

    def share(i):
        if i == 0:
            src = wave.at[:, yh]
        else:
            src = waves.at[1 - yh, core]
            settle(*(("got", "w", p) for p in range(X)))
        q = yh if i == 0 else 1 - yh
        start(("s", i), src, waves.at[q, core], s_send.at[i], s_recv.at[i], sibling, waves.at[q, 1 - core])

    def wave_ready(_):
        own_wave.wait()
        settle(("got", "s", 0), ("got", "s", 1))
        for p in range(X):
            high, low = split(jnp.concatenate([waves[q // 2, q % 2, p] for q in range(4)], axis=1))
            wave_high[p] = high
            wave_low[p] = low

    def scatter(key, count, piece, send, recv, whole, may_be_here):
        @pl.loop(0, count)
        def _(i):
            src, dst, to, here = piece(i)

            @pl.when(jnp.logical_not(here))
            def _():
                remote(src, dst, send, recv, to).start()

            @pl.when(here)
            def _():
                pltpu.make_async_copy(src, dst, recv).start()

        def sent():
            @pl.when(may_be_here)
            def _():
                wait(whole.at[pl.ds(0, count - 1)], send)

            @pl.when(jnp.logical_not(may_be_here))
            def _():
                wait(whole, send)

        owed[("sent", *key)] = sent
        owed[("got", *key)] = lambda: wait(whole, recv)

    def forward(h):
        settle(("got", "a", h))
        if GATE_B:
            settle(("sent", "b", h - 1))

        def piece(i):
            j = (i + row // 2) % (2 * X)
            from_x, to_yh = j // 2, j % 2
            src = spread.at[h, from_x, :, pl.ds(pl.multiple_of(to_yh * 256, 256), 256)]
            to = device(to_yh, yh, x, 2 * from_x + core, z % 2)
            here = (yl == yh) & (to_yh == yh) & (2 * from_x + core == z)
            return src, gathered.at[h, x, row // 2], to, here

        scatter(("b", h), 2 * X, piece, b_send.at[h], b_recv.at[h], gathered.at[h, x], (yl == yh) & (z % 2 == core))

    from_left, from_right, far = ((x + s) % X for s in (3, 1, 2))
    half = n // 4

    def gather_own(h):
        settle(("got", "b", h))
        if GATE_O:
            settle(("sent", "g", h - 1, 0), ("sent", "g", h - 1, 1))
        own = gathered.at[h, x]
        start(("g", h, 0), own, own, g_send.at[h, 0], g_recv.at[h, 0], right, gathered.at[h, from_left])
        start(("g", h, 1), own, own, g_send.at[h, 1], g_recv.at[h, 1], left, gathered.at[h, from_right])
        if DIRECT:
            start(("g", h, 2), own, own, g_send.at[h, 2], g_recv.at[h, 2], opposite, gathered.at[h, far])

    def gather_relay(h):
        for i, slot, to, first in ((0, from_left, right, 0), (1, from_right, left, half)):
            settle(("got", "g", h, i))
            piece = gathered.at[h, slot, pl.ds(first, half)]
            landing = gathered.at[h, far, pl.ds(first, half)]
            start(("g", h, 2 + i), piece, piece, g_send.at[h, 2 + i], g_recv.at[h, 2 + i], to, landing)

    def multiply(h):
        settle(*(("got", "g", h, i) for i in range(4)))
        total = None
        size = n // 2 * height
        for p in range(X):
            high, low = split(gathered[h, p].reshape(size, 256))
            both = dot(jnp.concatenate([high, low], axis=0), wave_high[p])
            term = both[:size] + both[size:] + dot(high, wave_low[p])
            total = term if total is None else total + term
        for q in range(4):
            part[h, q // 2, q % 2] = total[:, q * 128 : (q + 1) * 128].reshape(n // 2, height, 128)
        start(("y", h), part.at[h, 1 - yh], other.at[h], y_send.at[h], y_recv.at[h], across)

    def reduce(h):
        settle(("got", "y", h))
        summed[h] = part[h, yh] + other[h]

        def piece(i):
            j = (i + row) % n
            to = 2 * (j // 2) + core
            here = (to == row) & (j % 2 == core)
            src = summed.at[h, j % 2, j // 2]
            return src, landed.at[h, row], (to, yh * 2 * X + x * 2 + j % 2), here

        scatter(("z", h), n, piece, z_send.at[h], z_recv.at[h], landed.at[h], row % 2 == core)

    steps = dict(A=spread_out, B=forward, O=gather_own, L=gather_relay, M=multiply, R=reduce, W=cross, S=share, V=wave_ready)
    for step in ORDER:
        steps[step[0]](int(step[1:]))

    if TRUNC:
        out[...] = mixing[:64]
        if "V0" not in ORDER: own_wave.wait()
        settle(*list(owed))
        return

    rows = []
    for h in range(chunks):
        settle(("got", "z", h))
        rows.append(jnp.sum(landed[h], axis=0))
    block = jnp.concatenate(rows + [jnp.zeros((128 - chunks * height, 128), jnp.float32)], axis=0)
    turned = lax.dot_general(
        mixing, block, (((1,), (1,)), ((), ())), precision=lax.Precision.HIGHEST, preferred_element_type=jnp.float32
    )
    mixed[...] = turned.reshape(mixed.shape)

    @pl.loop(1, n)
    def _(j):
        to = (col + j) % n
        remote(mixed.at[to], final.at[col], f_send, f_recv, (row, to)).start()

    final[col] = mixed[col]
    wait(final.at[pl.ds(0, n - 1)], f_recv)
    out[...] = final[...].reshape(size, 128).T[: chunks * height]

    wait(final.at[pl.ds(0, n - 1)], f_send)
    settle(*list(owed))


def shards(env, wave, mpo):
    n = lax.axis_size("row")
    rows, depth = env.shape
    height = rows // CHUNKS
    wave4 = wave.reshape(X, 2, depth // (2 * X), wave.shape[1])
    f32, bf16 = jnp.float32, jnp.bfloat16
    dma = pltpu.SemaphoreType.DMA
    h = CHUNKS
    return pl.pallas_call(
        kernel,
        out_shape=jax.ShapeDtypeStruct((rows, 128), f32),
        in_specs=[
            pl.BlockSpec(memory_space=pltpu.HBM),
            pl.BlockSpec(memory_space=pltpu.HBM),
            pl.BlockSpec(memory_space=pltpu.HBM),
        ],
        out_specs=pl.BlockSpec(memory_space=pltpu.VMEM),
        scratch_shapes=[
            pltpu.VMEM((h, X, height, depth // X), f32),
            pltpu.VMEM((h, X, n // 2, height, 256), f32),
            pltpu.VMEM((2, 2, X, depth // (2 * X), 128), f32),
            pltpu.VMEM((X, depth // (2 * X), 512), bf16),
            pltpu.VMEM((X, depth // (2 * X), 512), bf16),
            pltpu.VMEM((h, 2, 2, n // 2, height, 128), f32),
            pltpu.VMEM((h, 2, n // 2, height, 128), f32),
            pltpu.VMEM((h, 2, n // 2, height, 128), f32),
            pltpu.VMEM((h, n, height, 128), f32),
            pltpu.VMEM((n, 8, 128), f32),
            pltpu.VMEM((n, 8, 128), f32),
            pltpu.VMEM(mpo.shape, f32),
            dma((h,)), dma((h,)), dma((h,)), dma((h,)), dma((X,)), dma((X,)), dma((2,)), dma((2,)), dma((h, 4)), dma((h, 4)),
            dma((h,)), dma((h,)), dma((h,)), dma((h,)), dma, dma, dma, dma,
        ],
        compiler_params=pltpu.CompilerParams(
            collective_id=0, has_side_effects=True, vmem_limit_bytes=40 * 1024 * 1024
        ),
    )(env, wave4, mpo)


def solution(mesh):
    in_specs = (P("row", "col"), P("row", "col"), P())
    out_specs = P("row", "col")
    return jax.shard_map(shards, mesh=mesh, in_specs=in_specs, out_specs=out_specs, check_vma=False)
```

time: 84.7 us -> 75 us (0.89)
  Pallas kernels: 80.9 us -> 71.2 us
    pallas_call x1, Pallas kernels: 80.9 us -> 71.2 us  [shards(): pl.pallas_call(kernel, out_shape=jax.ShapeDtypeStruct((rows, 128), f32),...]
where the time goes in v3:
time: 75 us; the launch traced here: 74.8 us
  Pallas kernels  71.2 us (95%)
  local copies, waits for them, and re-layouts  3.58 us (5%)
    pallas_call x1, Pallas kernels, shards(): pl.pallas_call(kernel, out_shape=jax.ShapeDtypeStruct((rows, 128), f32),...  71.2 us
    unnamed x7, local copies, waits for them, and re-layouts  3.58 us

profile of v3, /device:TPU:1, one launch (start us, length us, event | category | flops | bytes accessed | tf_op | source)
XLA Modules:
  0.0 74.8 jit_solution(5707057020739966402)
XLA Ops:
  0.0 0.0 copy-start
  0.0 1.2 %copy-done = f32[2048,128]{1,0:T(8,128)S(1)} copy-done((f32[2048,128]{1,0:T(8,128)S(1)}, f32[2048,128]{1,0:T(8,128)}, u32[]{:S(2)}) %copy-start) | copy-done | bytes 1048600
  1.2 0.0 copy-start.1
  1.2 1.0 %copy-done.1 = f32[64,2048]{1,0:T(8,128)S(1)} copy-done((f32[64,2048]{1,0:T(8,128)S(1)}, f32[64,2048]{1,0:T(8,128)}, u32[]{:S(2)}) %copy-start.1) | copy-done | bytes 524312
  2.3 0.0 copy-start.2
  2.3 0.7 copy-done.2
  3.0 71.2 %shard_map.37 = f32[64,128]{1,0:T(8,128)S(1)} custom-call(f32[64,2048]{1,0:T(8,128)S(1)} %copy-done.1, f32[4,2,256,128]{3,2,1,0:T(8,128)S(1)} %bitcast.1, f32[16,16]{1,0:T(8,128)S(1)} %copy-done.2), custom_call_target="tpu_custom_call" | custom-call | tf_op jit(solution)/shard_map/pallas_call | solution.py:288
  74.1 0.6 copy.5
Async XLA Ops:
  0.0 1.2 %copy-start = (f32[2048,128]{1,0:T(8,128)S(1)}, f32[2048,128]{1,0:T(8,128)}, u32[]{:S(2)}) copy-start(f32[2048,128]{1,0:T(8,128)} %param.4) | copy-start | bytes 3145732
  1.2 1.0 %copy-start.1 = (f32[64,2048]{1,0:T(8,128)S(1)}, f32[64,2048]{1,0:T(8,128)}, u32[]{:S(2)}) copy-start(f32[64,2048]{1,0:T(8,128)} %env.1) | copy-start | bytes 1572868
  2.3 0.7 copy-start.2

commit v4 on v3

v4 whole, which is shorter than its diff:
```python
import itertools

import jax
import jax.numpy as jnp
from jax import lax
from jax.experimental import pallas as pl
from jax.experimental.pallas import tpu as pltpu
from jax.sharding import PartitionSpec as P

MESH = pl.DeviceIdType.MESH
HEIGHTS = (24, 16, 16, 8)
GATED = (1, 2)
ORDER = (
    "W0", "W1", "A0", "W2", "W3", "S0", "A1", "B0", "A2",
    "A3", "B1", "O0", "B2", "O1", "B3", "S1", "V0", "O2",
    "M0", "O3", "M1", "R0", "M2", "R1", "M3", "R2", "R3",
)
X, Z = 4, 8


def device(yh, yl, x, z, core):
    return (yl * Z + z, yh * 2 * X + x * 2 + core)


def wrap(i, n):
    return jnp.where(i >= n, i - n, i)


def split(value):
    high = value.astype(jnp.bfloat16)
    return high, (value - high.astype(jnp.float32)).astype(jnp.bfloat16)


def dot(a, b):
    return jnp.dot(a, b, preferred_element_type=jnp.float32)


def kernel(
    env, wave, mpo, out, spread, gathered, waves, wave_high, wave_low, part, other, summed, landed, mixed, final, table,
    a_send, a_recv, b_send, b_recv, w_send, w_recv, s_send, s_recv, g_send, g_recv, y_send, y_recv, z_send, z_recv,
    f_send, f_recv, w_local, t_local,
):
    row, col = lax.axis_index("row"), lax.axis_index("col")
    yl, yh = jnp.where(row >= Z, 1, 0), jnp.where(col >= 2 * X, 1, 0)
    z = row - yl * Z
    x, core = lax.div(col, 2) - yh * X, lax.rem(col, 2)
    zh, zl = lax.div(z, 2), lax.rem(z, 2)
    chunks = len(landed)
    n = landed[0].shape[0]
    heights = [ref.shape[1] for ref in landed]
    firsts = [sum(heights[:h]) for h in range(chunks)]

    def remote(src, dst, send, recv, to):
        return pltpu.make_async_remote_copy(
            src_ref=src, dst_ref=dst, send_sem=send, recv_sem=recv, device_id=to, device_id_type=MESH
        )

    def wait(ref, sem):
        pltpu.make_async_copy(ref, ref, sem).wait()

    right = device(yh, yl, wrap(x + 1, X), z, core)
    left = device(yh, yl, wrap(x + X - 1, X), z, core)
    opposite = device(yh, yl, wrap(x + 2, X), z, core)
    sibling = device(yh, yl, x, z, 1 - core)
    across = device(1 - yh, yl, x, z, core)

    barrier = pltpu.get_barrier_semaphore()

    def greet(to):
        pl.semaphore_signal(barrier, inc=1, device_id=to, device_id_type=MESH)

    for step in range(1, X):
        greet(device(yh, yl, wrap(x + step, X), z, core))
    greet(sibling)
    greet(across)
    source = yl * 2 * X + x * 2 + zl
    reducer = yh * 2 * X + x * 2 + zl

    @pl.loop(0, n // 2)
    def _(j):
        greet((2 * j + core, source))

    @pl.loop(0, n)
    def _(j):
        greet((j, reducer))

    @pl.loop(1, n)
    def _(j):
        greet((row, wrap(col + j, n)))

    own_table = pltpu.make_async_copy(mpo, table, t_local)
    own_table.start()
    own_wave = pltpu.make_async_copy(wave.at[:, yh], waves.at[yh, core], w_local)
    own_wave.start()

    own_table.wait()
    spins = mpo.shape[0]
    size = mixed.shape[0] * mixed.shape[1]
    rights = size // spins
    wide = lax.broadcasted_iota(jnp.int32, (size, spins), 0)
    pick_t = (wide // rights == lax.broadcasted_iota(jnp.int32, (size, spins), 1)).astype(jnp.float32)
    tall = lax.broadcasted_iota(jnp.int32, (spins, size), 1)
    pick_s = (tall % spins == lax.broadcasted_iota(jnp.int32, (spins, size), 0)).astype(jnp.float32)
    by_t = lax.dot_general(
        pick_t, table[...], (((1,), (1,)), ((), ())), precision=lax.Precision.HIGHEST,
        preferred_element_type=jnp.float32,
    )
    full = jnp.dot(by_t, pick_s, precision=lax.Precision.HIGHEST, preferred_element_type=jnp.float32)
    same = (
        lax.broadcasted_iota(jnp.int32, (size, size), 0) % rights
        == lax.broadcasted_iota(jnp.int32, (size, size), 1) // spins
    )
    mixing = jnp.where(same, full, 0.0)

    pl.semaphore_wait(barrier, (X - 1) + 2 + n // 2 + n + (n - 1))

    wide_k = spread[0].shape[2]

    def slices(h, to_x):
        return env.at[pl.ds(firsts[h], heights[h]), pl.ds(pl.multiple_of(to_x * wide_k, wide_k), wide_k)]

    owed = {}

    def settle(*keys):
        for key in keys:
            if key in owed:
                owed.pop(key)()

    def start(key, src, dst, send, recv, to, landing=None):
        remote(src, dst, send, recv, to).start()
        owed[("sent", *key)] = lambda: wait(src, send)
        owed[("got", *key)] = lambda: wait(dst if landing is None else landing, recv)

    def spread_out(h):
        settle(("sent", "a", h - 1))
        for step in range(1, X):
            to_x = wrap(x + step, X)
            to = device(yh, yl, to_x, z, core)
            remote(slices(h, to_x), spread[h].at[x], a_send.at[h], a_recv.at[h], to).start()
        pltpu.make_async_copy(slices(h, x), spread[h].at[x], a_recv.at[h]).start()
        owed["sent", "a", h] = lambda: wait(spread[h].at[pl.ds(0, X - 1)], a_send.at[h])
        owed["got", "a", h] = lambda: wait(spread[h], a_recv.at[h])

    def cross(p):
        dst = waves.at[yh, core, p]
        start(("w", p), wave.at[p, 1 - yh], dst, w_send.at[p], w_recv.at[p], across, waves.at[1 - yh, core, p])

    def share(i):
        if i == 0:
            src = wave.at[:, yh]
        else:
            src = waves.at[1 - yh, core]
            settle(*(("got", "w", p) for p in range(X)))
        q = yh if i == 0 else 1 - yh
        start(("s", i), src, waves.at[q, core], s_send.at[i], s_recv.at[i], sibling, waves.at[q, 1 - core])

    def wave_ready(_):
        own_wave.wait()
        settle(("got", "s", 0), ("got", "s", 1))
        for p in range(X):
            high, low = split(jnp.concatenate([waves[q // 2, q % 2, p] for q in range(4)], axis=1))
            wave_high[p] = high
            wave_low[p] = low

    def scatter(key, count, piece, send, recv, whole, may_be_here):
        @pl.loop(0, X)
        def _(i):
            for src, dst, to, here in piece(i):
                @pl.when(jnp.logical_not(here))
                def _():
                    remote(src, dst, send, recv, to).start()

                @pl.when(here)
                def _():
                    pltpu.make_async_copy(src, dst, recv).start()

        def sent():
            @pl.when(may_be_here)
            def _():
                wait(whole.at[pl.ds(0, count - 1)], send)

            @pl.when(jnp.logical_not(may_be_here))
            def _():
                wait(whole, send)

        owed[("sent", *key)] = sent
        owed[("got", *key)] = lambda: wait(whole, recv)

    def forward(h):
        settle(("got", "a", h))
        settle(("sent", "b", h - 1))

        def piece(i):
            from_x = wrap(zh + i, X)
            for to_yh in range(2):
                src = spread[h].at[from_x, :, pl.ds(to_yh * 256, 256)]
                here = (yl == yh) & (to_yh == yh) & (2 * from_x + core == z)
                yield src, gathered[h].at[x, yl * X + zh], device(to_yh, yh, x, 2 * from_x + core, zl), here

        scatter(("b", h), 2 * X, piece, b_send.at[h], b_recv.at[h], gathered[h].at[x], (yl == yh) & (zl == core))

    from_left, from_right, far = (wrap(x + s, X) for s in (3, 1, 2))

    def gather_own(h):
        settle(("got", "b", h))
        if h in GATED:
            settle(("sent", "g", h - 1, 0), ("sent", "g", h - 1, 1))
        own = gathered[h].at[x]
        start(("g", h, 0), own, own, g_send.at[h, 0], g_recv.at[h, 0], right, gathered[h].at[from_left])
        start(("g", h, 1), own, own, g_send.at[h, 1], g_recv.at[h, 1], left, gathered[h].at[from_right])
        start(("g", h, 2), own, own, g_send.at[h, 2], g_recv.at[h, 2], opposite, gathered[h].at[far])

    def multiply(h):
        settle(*(("got", "g", h, i) for i in range(3)))
        total = None
        height = heights[h]
        size = n // 2 * height
        for p in range(X):
            high, low = split(gathered[h][p].reshape(size, 256))
            both = dot(jnp.concatenate([high, low], axis=0), wave_high[p])
            term = both[:size] + both[size:] + dot(high, wave_low[p])
            total = term if total is None else total + term
        for q in range(4):
            part[h][q // 2, q % 2] = total[:, q * 128 : (q + 1) * 128].reshape(n // 2, height, 128)
        start(("y", h), part[h].at[1 - yh], other[h], y_send.at[h], y_recv.at[h], across)

    def reduce(h):
        settle(("got", "y", h))
        summed[h][...] = part[h][yh] + other[h][...]

        def piece(i):
            zz = wrap(zh + i, X)
            for to_yl, to_core in itertools.product(range(2), repeat=2):
                src = summed[h].at[to_core, to_yl * X + zz]
                here = (2 * zz + core == z) & (to_yl == yl) & (to_core == core)
                yield src, landed[h].at[row], device(yh, to_yl, x, 2 * zz + core, to_core), here

        scatter(("z", h), n, piece, z_send.at[h], z_recv.at[h], landed[h], zl == core)

    steps = dict(A=spread_out, B=forward, O=gather_own, M=multiply, R=reduce, W=cross, S=share, V=wave_ready)
    for step in ORDER:
        steps[step[0]](int(step[1:]))

    rows = []
    for h in range(chunks):
        settle(("got", "z", h))
        rows.append(jnp.sum(landed[h][...], axis=0))
    block = jnp.concatenate(rows + [jnp.zeros((128 - sum(heights), 128), jnp.float32)], axis=0)
    turned = lax.dot_general(
        mixing, block, (((1,), (1,)), ((), ())), precision=lax.Precision.HIGHEST, preferred_element_type=jnp.float32
    )
    mixed[...] = turned.reshape(mixed.shape)

    @pl.loop(1, n)
    def _(j):
        to = wrap(col + j, n)
        remote(mixed.at[to], final.at[col], f_send, f_recv, (row, to)).start()

    final[col] = mixed[col]
    wait(final.at[pl.ds(0, n - 1)], f_recv)
    out[...] = final[...].reshape(size, 128).T[: sum(heights)]

    wait(final.at[pl.ds(0, n - 1)], f_send)
    settle(*list(owed))


def shards(env, wave, mpo):
    n = lax.axis_size("row")
    rows, depth = env.shape
    wave4 = wave.reshape(X, 2, depth // (2 * X), wave.shape[1])
    f32, bf16 = jnp.float32, jnp.bfloat16
    dma = pltpu.SemaphoreType.DMA
    h = len(HEIGHTS)
    return pl.pallas_call(
        kernel,
        out_shape=jax.ShapeDtypeStruct((rows, 128), f32),
        in_specs=[
            pl.BlockSpec(memory_space=pltpu.HBM),
            pl.BlockSpec(memory_space=pltpu.HBM),
            pl.BlockSpec(memory_space=pltpu.HBM),
        ],
        out_specs=pl.BlockSpec(memory_space=pltpu.VMEM),
        scratch_shapes=[
            [pltpu.VMEM((X, height, depth // X), f32) for height in HEIGHTS],
            [pltpu.VMEM((X, n // 2, height, 256), f32) for height in HEIGHTS],
            pltpu.VMEM((2, 2, X, depth // (2 * X), 128), f32),
            pltpu.VMEM((X, depth // (2 * X), 512), bf16),
            pltpu.VMEM((X, depth // (2 * X), 512), bf16),
            [pltpu.VMEM((2, 2, n // 2, height, 128), f32) for height in HEIGHTS],
            [pltpu.VMEM((2, n // 2, height, 128), f32) for height in HEIGHTS],
            [pltpu.VMEM((2, n // 2, height, 128), f32) for height in HEIGHTS],
            [pltpu.VMEM((n, height, 128), f32) for height in HEIGHTS],
            pltpu.VMEM((n, 8, 128), f32),
            pltpu.VMEM((n, 8, 128), f32),
            pltpu.VMEM(mpo.shape, f32),
            dma((h,)), dma((h,)), dma((h,)), dma((h,)), dma((X,)), dma((X,)), dma((2,)), dma((2,)), dma((h, 3)), dma((h, 3)),
            dma((h,)), dma((h,)), dma((h,)), dma((h,)), dma, dma, dma, dma,
        ],
        compiler_params=pltpu.CompilerParams(
            collective_id=0, has_side_effects=True, vmem_limit_bytes=40 * 1024 * 1024
        ),
    )(env, wave4, mpo)


def solution(mesh):
    in_specs = (P("row", "col"), P("row", "col"), P())
    out_specs = P("row", "col")
    return jax.shard_map(shards, mesh=mesh, in_specs=in_specs, out_specs=out_specs, check_vma=False)
```

time: 75 us -> 73.4 us (0.979)
  Pallas kernels: 71.2 us -> 69.6 us
    pallas_call x1, Pallas kernels: 71.2 us -> 69.6 us  [shards(): pl.pallas_call(kernel, out_shape=jax.ShapeDtypeStruct((rows, 128), f32),...]
where the time goes in v4:
time: 73.4 us; the launch traced here: 73.2 us
  Pallas kernels  69.6 us (95%)
  local copies, waits for them, and re-layouts  3.58 us (5%)
    pallas_call x1, Pallas kernels, shards(): pl.pallas_call(kernel, out_shape=jax.ShapeDtypeStruct((rows, 128), f32),...  69.6 us
    unnamed x7, local copies, waits for them, and re-layouts  3.58 us

profile of v4, /device:TPU:1, one launch (start us, length us, event | category | flops | bytes accessed | tf_op | source)
XLA Modules:
  0.0 73.2 jit_solution(9840964964006678564)
XLA Ops:
  0.0 0.0 copy-start
  0.0 1.2 %copy-done = f32[2048,128]{1,0:T(8,128)S(1)} copy-done((f32[2048,128]{1,0:T(8,128)S(1)}, f32[2048,128]{1,0:T(8,128)}, u32[]{:S(2)}) %copy-start) | copy-done | bytes 1048600
  1.2 0.0 copy-start.1
  1.2 1.0 %copy-done.1 = f32[64,2048]{1,0:T(8,128)S(1)} copy-done((f32[64,2048]{1,0:T(8,128)S(1)}, f32[64,2048]{1,0:T(8,128)}, u32[]{:S(2)}) %copy-start.1) | copy-done | bytes 524312
  2.3 0.0 copy-start.2
  2.3 0.7 copy-done.2
  3.0 69.6 %shard_map.37 = f32[64,128]{1,0:T(8,128)S(1)} custom-call(f32[64,2048]{1,0:T(8,128)S(1)} %copy-done.1, f32[4,2,256,128]{3,2,1,0:T(8,128)S(1)} %bitcast.1, f32[16,16]{1,0:T(8,128)S(1)} %copy-done.2), custom_call_target="tpu_custom_call" | custom-call | tf_op jit(solution)/shard_map/pallas_call | solution.py:274
  72.6 0.6 copy.5
Async XLA Ops:
  0.0 1.2 %copy-start = (f32[2048,128]{1,0:T(8,128)S(1)}, f32[2048,128]{1,0:T(8,128)}, u32[]{:S(2)}) copy-start(f32[2048,128]{1,0:T(8,128)} %param.4) | copy-start | bytes 3145732
  1.2 1.0 %copy-start.1 = (f32[64,2048]{1,0:T(8,128)S(1)}, f32[64,2048]{1,0:T(8,128)}, u32[]{:S(2)}) copy-start(f32[64,2048]{1,0:T(8,128)} %env.1) | copy-start | bytes 1572868
  2.3 0.7 copy-start.2

commit v5 on v4

--- a/solution.py
+++ b/solution.py
@@ -13,7 +13,7 @@
 ORDER = (
     "W0", "W1", "A0", "W2", "W3", "S0", "A1", "B0", "A2",
     "A3", "B1", "O0", "B2", "O1", "B3", "S1", "V0", "O2",
-    "M0", "O3", "M1", "R0", "M2", "R1", "M3", "R2", "R3",
+    "M0", "O3", "M1", "M2", "R0", "M3", "R1", "R2", "R3",
 )
 X, Z = 4, 8
 

time: 73.4 us -> 73.3 us (level)
  no operation moved by 1% of the time
where the time goes in v5:
time: 73.3 us; the launch traced here: 73.1 us
  Pallas kernels  69.5 us (95%)
  local copies, waits for them, and re-layouts  3.58 us (5%)
    pallas_call x1, Pallas kernels, shards(): pl.pallas_call(kernel, out_shape=jax.ShapeDtypeStruct((rows, 128), f32),...  69.5 us
    unnamed x7, local copies, waits for them, and re-layouts  3.58 us

profile of v5, /device:TPU:1, one launch (start us, length us, event | category | flops | bytes accessed | tf_op | source)
XLA Modules:
  0.0 73.1 jit_solution(560666401622787420)
XLA Ops:
  0.0 0.0 copy-start
  0.0 1.2 %copy-done = f32[2048,128]{1,0:T(8,128)S(1)} copy-done((f32[2048,128]{1,0:T(8,128)S(1)}, f32[2048,128]{1,0:T(8,128)}, u32[]{:S(2)}) %copy-start) | copy-done | bytes 1048600
  1.2 0.0 copy-start.1
  1.2 1.0 %copy-done.1 = f32[64,2048]{1,0:T(8,128)S(1)} copy-done((f32[64,2048]{1,0:T(8,128)S(1)}, f32[64,2048]{1,0:T(8,128)}, u32[]{:S(2)}) %copy-start.1) | copy-done | bytes 524312
  2.3 0.0 copy-start.2
  2.3 0.7 copy-done.2
  3.0 69.5 %shard_map.37 = f32[64,128]{1,0:T(8,128)S(1)} custom-call(f32[64,2048]{1,0:T(8,128)S(1)} %copy-done.1, f32[4,2,256,128]{3,2,1,0:T(8,128)S(1)} %bitcast.1, f32[16,16]{1,0:T(8,128)S(1)} %copy-done.2), custom_call_target="tpu_custom_call" | custom-call | tf_op jit(solution)/shard_map/pallas_call | solution.py:274
  72.5 0.6 copy.5
Async XLA Ops:
  0.0 1.2 %copy-start = (f32[2048,128]{1,0:T(8,128)S(1)}, f32[2048,128]{1,0:T(8,128)}, u32[]{:S(2)}) copy-start(f32[2048,128]{1,0:T(8,128)} %param.4) | copy-start | bytes 3145732
  1.2 1.0 %copy-start.1 = (f32[64,2048]{1,0:T(8,128)S(1)}, f32[64,2048]{1,0:T(8,128)}, u32[]{:S(2)}) copy-start(f32[64,2048]{1,0:T(8,128)} %env.1) | copy-start | bytes 1572868
  2.3 0.7 copy-start.2

commit v6 on v5

--- a/solution.py
+++ b/solution.py
@@ -92,6 +92,135 @@
     own_table.start()
     own_wave = pltpu.make_async_copy(wave.at[:, yh], waves.at[yh, core], w_local)
     own_wave.start()
+
+    pl.semaphore_wait(barrier, (X - 1) + 2 + n // 2 + n + (n - 1))
+
+    wide_k = spread[0].shape[2]
+
+    def slices(h, to_x):
+        return env.at[pl.ds(firsts[h], heights[h]), pl.ds(pl.multiple_of(to_x * wide_k, wide_k), wide_k)]
+
+    owed = {}
+
+    def settle(*keys):
+        for key in keys:
+            if key in owed:
+                owed.pop(key)()
+
+    def start(key, src, dst, send, recv, to, landing=None):
+        remote(src, dst, send, recv, to).start()
+        owed[("sent", *key)] = lambda: wait(src, send)
+        owed[("got", *key)] = lambda: wait(dst if landing is None else landing, recv)
+
+    def spread_out(h):
+        settle(("sent", "a", h - 1))
+        for step in range(1, X):
+            to_x = wrap(x + step, X)
+            to = device(yh, yl, to_x, z, core)
+            remote(slices(h, to_x), spread[h].at[x], a_send.at[h], a_recv.at[h], to).start()
+        pltpu.make_async_copy(slices(h, x), spread[h].at[x], a_recv.at[h]).start()
+        owed["sent", "a", h] = lambda: wait(spread[h].at[pl.ds(0, X - 1)], a_send.at[h])
+        owed["got", "a", h] = lambda: wait(spread[h], a_recv.at[h])
+
+    def cross(p):
+        dst = waves.at[yh, core, p]
+        start(("w", p), wave.at[p, 1 - yh], dst, w_send.at[p], w_recv.at[p], across, waves.at[1 - yh, core, p])
+
+    def share(i):
+        if i == 0:
+            src = wave.at[:, yh]
+        else:
+            src = waves.at[1 - yh, core]
+            settle(*(("got", "w", p) for p in range(X)))
+        q = yh if i == 0 else 1 - yh
+        start(("s", i), src, waves.at[q, core], s_send.at[i], s_recv.at[i], sibling, waves.at[q, 1 - core])
+
+    def wave_ready(_):
+        own_wave.wait()
+        settle(("got", "s", 0), ("got", "s", 1))
+        for p in range(X):
+            high, low = split(jnp.concatenate([waves[q // 2, q % 2, p] for q in range(4)], axis=1))
+            wave_high[p] = high
+            wave_low[p] = low
+
+    def scatter(key, count, piece, send, recv, whole, may_be_here):
+        @pl.loop(0, X)
+        def _(i):
+            for src, dst, to, here in piece(i):
+                @pl.when(jnp.logical_not(here))
+                def _():
+                    remote(src, dst, send, recv, to).start()
+
+                @pl.when(here)
+                def _():
+                    pltpu.make_async_copy(src, dst, recv).start()
+
+        def sent():
+            @pl.when(may_be_here)
+            def _():
+                wait(whole.at[pl.ds(0, count - 1)], send)
+
+            @pl.when(jnp.logical_not(may_be_here))
+            def _():
+                wait(whole, send)
+
+        owed[("sent", *key)] = sent
+        owed[("got", *key)] = lambda: wait(whole, recv)
+
+    def forward(h):
+        settle(("got", "a", h))
+        settle(("sent", "b", h - 1))
+
+        def piece(i):
+            from_x = wrap(zh + i, X)
+            for to_yh in range(2):
+                src = spread[h].at[from_x, :, pl.ds(to_yh * 256, 256)]
+                here = (yl == yh) & (to_yh == yh) & (2 * from_x + core == z)
+                yield src, gathered[h].at[x, yl * X + zh], device(to_yh, yh, x, 2 * from_x + core, zl), here
+
+        scatter(("b", h), 2 * X, piece, b_send.at[h], b_recv.at[h], gathered[h].at[x], (yl == yh) & (zl == core))
+
+    from_left, from_right, far = (wrap(x + s, X) for s in (3, 1, 2))
+
+    def gather_own(h):
+        settle(("got", "b", h))
+        if h in GATED:
+            settle(("sent", "g", h - 1, 0), ("sent", "g", h - 1, 1))
+        own = gathered[h].at[x]
+        start(("g", h, 0), own, own, g_send.at[h, 0], g_recv.at[h, 0], right, gathered[h].at[from_left])
+        start(("g", h, 1), own, own, g_send.at[h, 1], g_recv.at[h, 1], left, gathered[h].at[from_right])
+        start(("g", h, 2), own, own, g_send.at[h, 2], g_recv.at[h, 2], opposite, gathered[h].at[far])
+
+    def multiply(h):
+        settle(*(("got", "g", h, i) for i in range(3)))
+        total = None
+        height = heights[h]
+        size = n // 2 * height
+        for p in range(X):
+            high, low = split(gathered[h][p].reshape(size, 256))
+            both = dot(jnp.concatenate([high, low], axis=0), wave_high[p])
+            term = both[:size] + both[size:] + dot(high, wave_low[p])
+            total = term if total is None else total + term
+        for q in range(4):
+            part[h][q // 2, q % 2] = total[:, q * 128 : (q + 1) * 128].reshape(n // 2, height, 128)
+        start(("y", h), part[h].at[1 - yh], other[h], y_send.at[h], y_recv.at[h], across)
+
+    def reduce(h):
+        settle(("got", "y", h))
+        summed[h][...] = part[h][yh] + other[h][...]
+
+        def piece(i):
+            zz = wrap(zh + i, X)
+            for to_yl, to_core in itertools.product(range(2), repeat=2):
+                src = summed[h].at[to_core, to_yl * X + zz]
+                here = (2 * zz + core == z) & (to_yl == yl) & (to_core == core)
+                yield src, landed[h].at[row], device(yh, to_yl, x, 2 * zz + core, to_core), here
+
+        scatter(("z", h), n, piece, z_send.at[h], z_recv.at[h], landed[h], zl == core)
+
+    steps = dict(A=spread_out, B=forward, O=gather_own, M=multiply, R=reduce, W=cross, S=share, V=wave_ready)
+    for step in ORDER:
+        steps[step[0]](int(step[1:]))
 
     own_table.wait()
     spins = mpo.shape[0]
@@ -111,135 +240,6 @@
         == lax.broadcasted_iota(jnp.int32, (size, size), 1) // spins
     )
     mixing = jnp.where(same, full, 0.0)
-
-    pl.semaphore_wait(barrier, (X - 1) + 2 + n // 2 + n + (n - 1))
-
-    wide_k = spread[0].shape[2]
-
-    def slices(h, to_x):
-        return env.at[pl.ds(firsts[h], heights[h]), pl.ds(pl.multiple_of(to_x * wide_k, wide_k), wide_k)]
-
-    owed = {}
-
-    def settle(*keys):
-        for key in keys:
-            if key in owed:
-                owed.pop(key)()
-
-    def start(key, src, dst, send, recv, to, landing=None):
-        remote(src, dst, send, recv, to).start()
-        owed[("sent", *key)] = lambda: wait(src, send)
-        owed[("got", *key)] = lambda: wait(dst if landing is None else landing, recv)
-
-    def spread_out(h):
-        settle(("sent", "a", h - 1))
-        for step in range(1, X):
-            to_x = wrap(x + step, X)
-            to = device(yh, yl, to_x, z, core)
-            remote(slices(h, to_x), spread[h].at[x], a_send.at[h], a_recv.at[h], to).start()
-        pltpu.make_async_copy(slices(h, x), spread[h].at[x], a_recv.at[h]).start()
-        owed["sent", "a", h] = lambda: wait(spread[h].at[pl.ds(0, X - 1)], a_send.at[h])
-        owed["got", "a", h] = lambda: wait(spread[h], a_recv.at[h])
-
-    def cross(p):
-        dst = waves.at[yh, core, p]
-        start(("w", p), wave.at[p, 1 - yh], dst, w_send.at[p], w_recv.at[p], across, waves.at[1 - yh, core, p])
-
-    def share(i):
-        if i == 0:
-            src = wave.at[:, yh]
-        else:
-            src = waves.at[1 - yh, core]
-            settle(*(("got", "w", p) for p in range(X)))
-        q = yh if i == 0 else 1 - yh
-        start(("s", i), src, waves.at[q, core], s_send.at[i], s_recv.at[i], sibling, waves.at[q, 1 - core])
-
-    def wave_ready(_):
-        own_wave.wait()
-        settle(("got", "s", 0), ("got", "s", 1))
-        for p in range(X):
-            high, low = split(jnp.concatenate([waves[q // 2, q % 2, p] for q in range(4)], axis=1))
-            wave_high[p] = high
-            wave_low[p] = low
-
-    def scatter(key, count, piece, send, recv, whole, may_be_here):
-        @pl.loop(0, X)
-        def _(i):
-            for src, dst, to, here in piece(i):
-                @pl.when(jnp.logical_not(here))
-                def _():
-                    remote(src, dst, send, recv, to).start()
-
-                @pl.when(here)
-                def _():
-                    pltpu.make_async_copy(src, dst, recv).start()
-
-        def sent():
-            @pl.when(may_be_here)
-            def _():
-                wait(whole.at[pl.ds(0, count - 1)], send)
-
-            @pl.when(jnp.logical_not(may_be_here))
-            def _():
-                wait(whole, send)
-
-        owed[("sent", *key)] = sent
-        owed[("got", *key)] = lambda: wait(whole, recv)
-
-    def forward(h):
-        settle(("got", "a", h))
-        settle(("sent", "b", h - 1))
-
-        def piece(i):
-            from_x = wrap(zh + i, X)
-            for to_yh in range(2):
-                src = spread[h].at[from_x, :, pl.ds(to_yh * 256, 256)]
-                here = (yl == yh) & (to_yh == yh) & (2 * from_x + core == z)
-                yield src, gathered[h].at[x, yl * X + zh], device(to_yh, yh, x, 2 * from_x + core, zl), here
-
-        scatter(("b", h), 2 * X, piece, b_send.at[h], b_recv.at[h], gathered[h].at[x], (yl == yh) & (zl == core))
-
-    from_left, from_right, far = (wrap(x + s, X) for s in (3, 1, 2))
-
-    def gather_own(h):
-        settle(("got", "b", h))
-        if h in GATED:
-            settle(("sent", "g", h - 1, 0), ("sent", "g", h - 1, 1))
-        own = gathered[h].at[x]
-        start(("g", h, 0), own, own, g_send.at[h, 0], g_recv.at[h, 0], right, gathered[h].at[from_left])
-        start(("g", h, 1), own, own, g_send.at[h, 1], g_recv.at[h, 1], left, gathered[h].at[from_right])
-        start(("g", h, 2), own, own, g_send.at[h, 2], g_recv.at[h, 2], opposite, gathered[h].at[far])
-
-    def multiply(h):
-        settle(*(("got", "g", h, i) for i in range(3)))
-        total = None
-        height = heights[h]
-        size = n // 2 * height
-        for p in range(X):
-            high, low = split(gathered[h][p].reshape(size, 256))
-            both = dot(jnp.concatenate([high, low], axis=0), wave_high[p])
-            term = both[:size] + both[size:] + dot(high, wave_low[p])
-            total = term if total is None else total + term
-        for q in range(4):
-            part[h][q // 2, q % 2] = total[:, q * 128 : (q + 1) * 128].reshape(n // 2, height, 128)
-        start(("y", h), part[h].at[1 - yh], other[h], y_send.at[h], y_recv.at[h], across)
-
-    def reduce(h):
-        settle(("got", "y", h))
-        summed[h][...] = part[h][yh] + other[h][...]
-
-        def piece(i):
-            zz = wrap(zh + i, X)
-            for to_yl, to_core in itertools.product(range(2), repeat=2):
-                src = summed[h].at[to_core, to_yl * X + zz]
-                here = (2 * zz + core == z) & (to_yl == yl) & (to_core == core)
-                yield src, landed[h].at[row], device(yh, to_yl, x, 2 * zz + core, to_core), here
-
-        scatter(("z", h), n, piece, z_send.at[h], z_recv.at[h], landed[h], zl == core)
-
-    steps = dict(A=spread_out, B=forward, O=gather_own, M=multiply, R=reduce, W=cross, S=share, V=wave_ready)
-    for step in ORDER:
-        steps[step[0]](int(step[1:]))
 
     rows = []
     for h in range(chunks):

time: 73.3 us -> 73.3 us (level)
  no operation moved by 1% of the time
where the time goes in v6:
time: 73.3 us; the launch traced here: 73.1 us
  Pallas kernels  69.5 us (95%)
  local copies, waits for them, and re-layouts  3.58 us (5%)
    pallas_call x1, Pallas kernels, shards(): pl.pallas_call(kernel, out_shape=jax.ShapeDtypeStruct((rows, 128), f32),...  69.5 us
    unnamed x7, local copies, waits for them, and re-layouts  3.58 us

profile of v6, /device:TPU:1, one launch (start us, length us, event | category | flops | bytes accessed | tf_op | source)
XLA Modules:
  0.0 73.1 jit_solution(13180828736885505464)
XLA Ops:
  0.0 0.0 copy-start
  0.0 1.2 %copy-done = f32[2048,128]{1,0:T(8,128)S(1)} copy-done((f32[2048,128]{1,0:T(8,128)S(1)}, f32[2048,128]{1,0:T(8,128)}, u32[]{:S(2)}) %copy-start) | copy-done | bytes 1048600
  1.2 0.0 copy-start.1
  1.2 1.0 %copy-done.1 = f32[64,2048]{1,0:T(8,128)S(1)} copy-done((f32[64,2048]{1,0:T(8,128)S(1)}, f32[64,2048]{1,0:T(8,128)}, u32[]{:S(2)}) %copy-start.1) | copy-done | bytes 524312
  2.3 0.0 copy-start.2
  2.3 0.7 copy-done.2
  3.0 69.5 %shard_map.37 = f32[64,128]{1,0:T(8,128)S(1)} custom-call(f32[64,2048]{1,0:T(8,128)S(1)} %copy-done.1, f32[4,2,256,128]{3,2,1,0:T(8,128)S(1)} %bitcast.1, f32[16,16]{1,0:T(8,128)S(1)} %copy-done.2), custom_call_target="tpu_custom_call" | custom-call | tf_op jit(solution)/shard_map/pallas_call | solution.py:274
  72.5 0.6 copy.5
Async XLA Ops:
  0.0 1.2 %copy-start = (f32[2048,128]{1,0:T(8,128)S(1)}, f32[2048,128]{1,0:T(8,128)}, u32[]{:S(2)}) copy-start(f32[2048,128]{1,0:T(8,128)} %param.4) | copy-start | bytes 3145732
  1.2 1.0 %copy-start.1 = (f32[64,2048]{1,0:T(8,128)S(1)}, f32[64,2048]{1,0:T(8,128)}, u32[]{:S(2)}) copy-start(f32[64,2048]{1,0:T(8,128)} %env.1) | copy-start | bytes 1572868
  2.3 0.7 copy-start.2
